TPU v7x, 32 devices: a whole 2x2x4 slice. The times are simulated.
32 devices in a mesh: worker: 4 (over x, core), outer: 4 (over z), mp: 2 (over y).
Axes of the slice: x: 2, y: 2, z: 4, core: 2. Of those that a mesh axis runs over, the one named last changes fastest.
Arguments:
- grads: float32 [4, 4, 3584, 4096], P('worker', 'outer', None, 'mp'), as said below
- center: float32 [3584, 4096], P(('worker', 'outer'), 'mp'), may hold values from -6 to 6
- radius: float32 [1], replicated, may hold values from 1.5 to 3.5
Outputs:
- center_out: float32 [3584, 4096], P(('worker', 'outer'), 'mp')
Inputs may be any that keep to these rules, and one draw needn't show every extreme that they name: `grads`: finite values.
All inputs are finite; a program needn't handle non-finite values.
Results may differ from a plain program's by a relative error of at most 0.0001.
Values sent between devices are 32-bit elements; how exact they have to be, the bound alone decides.
No kernel may reach another device: no remote copies, remote signals or barrier semaphores. Data moves between devices by JAX's collectives and lax.ppermute only.
A program may use at most 192 MiB of HBM per device.

v0:
```python
import math

import jax
import jax.numpy as jnp
from jax import lax
from jax.sharding import PartitionSpec as P

D = 3584
ITERS = 2
KVW = 4096


epsilon = 1e-06


def on_device(grads, center, radius):
    worker_count = lax.axis_size("worker") * lax.axis_size("outer")
    radius_total = radius[0] * math.sqrt(D * KVW)
    own_rows = center
    mine = grads.reshape(1, grads.shape[2], grads.shape[3])
    gathered = lax.all_to_all(mine, ("worker", "outer"), split_axis=1, concat_axis=0, tiled=True)
    for iteration in range(ITERS):
        difference = gathered - own_rows[None]
        partial_value = jnp.sum(difference * difference, axis=(1, 2))
        norm_sq = lax.psum(partial_value, ("worker", "outer", "mp"))
        factor = jnp.minimum(1.0, radius_total * lax.rsqrt(norm_sq + epsilon))
        summed = jnp.sum(factor[:, None, None] * difference, axis=0)
        own_rows = own_rows + summed / worker_count
    return own_rows


def solution(mesh):
    in_specs = (P("worker", "outer", None, "mp"), P(("worker", "outer"), "mp"), P())
    out_specs = P(("worker", "outer"), "mp")
    return jax.shard_map(
        on_device, mesh=mesh, in_specs=in_specs, out_specs=out_specs, check_vma=False
    )
```

profile of v0, /device:TPU:0, one launch (start us, length us, event | category | flops | bytes accessed | tf_op | source)
XLA Modules:
  0.0 934.4 jit_solution(12065390304282626729)
XLA Ops:
  0.0 23.7 %reshape.36 = f32[1,3584,2048]{2,0,1:T(1,128)} reshape(f32[1,1,3584,2048]{3,2,1,0:T(8,128)} %param.3) | data formatting | bytes 58720256 | tf_op jit(solution)/shard_map/reshape | solution.py:20
  23.7 0.0 copy-start.1
  23.7 7.6 all-to-all-start
  31.9 0.0 copy-done.1
  31.9 10.4 %sub.34 = f32[16,224,2048]{2,1,0:T(8,128)} broadcast(f32[224,2048]{1,0:T(8,128)S(1)} %copy-done.1), dimensions={1,2} | broadcast | bytes 31195136 | tf_op jit(solution)/shard_map/sub | solution.py:23
  42.3 42.5 %sub.35 = f32[1,3584,2048]{2,0,1:T(1,128)} reshape(f32[16,224,2048]{2,1,0:T(8,128)} %sub.34) | data formatting | bytes 58720256 | tf_op jit(solution)/shard_map/sub | solution.py:23
  84.8 580.0 %all-to-all-done = f32[1,3584,2048]{2,0,1:T(1,128)} async-done(((f32[1,3584,2048]{2,0,1:T(1,128)}), f32[1,3584,2048]{2,0,1:T(1,128)}, u32[]{:S(2)}, u32[]{:S(2)}) %all-to-all-start) | async-done | bytes 29360160 | tf_op jit(solution)/shard_map/all_to_all | solution.py:21
  664.9 45.4 %multiply_reduce_fusion.3 = f32[3584]{0:T(1024)S(1)} fusion(f32[1,3584,2048]{2,0,1:T(1,128)} %all-to-all-done, f32[1,3584,2048]{2,0,1:T(1,128)} %sub.35), kind=kLoop, calls=%fused_computation.3 | loop fusion | flops 22016512 | bytes 58734592 | tf_op jit(solution)/shard_map/reduce_sum | solution.py:24
  710.3 0.1 reduce_sum.43
  710.4 0.1 reduce_sum.52
  710.5 37.4 %psum.14 = f32[16]{0:T(128)S(1)} all-reduce(f32[16]{0:T(128)S(1)} %reduce_sum.52), channel_id=1, replica_groups=mesh['worker'=4,'outer'=4,'mp'=2] {'worker','outer','mp'}, use_global_device_ids=true, to_apply=%region_2.0 | all-reduce | flops 16 | bytes 128 | tf_op jit(solution)/shard_map/psum | solution.py:25
  747.9 17.7 %copy.4 = f32[1,3584,2048]{2,1,0:T(8,128)S(1)} copy(f32[1,3584,2048]{2,0,1:T(1,128)} %all-to-all-done) | data formatting | bytes 58720256
  765.6 0.0 copy-start
  765.6 0.0 copy-start.2
  765.6 10.3 %copy-done = f32[1,3584,2048]{2,1,0:T(8,128)} copy-done((f32[1,3584,2048]{2,1,0:T(8,128)}, f32[1,3584,2048]{2,1,0:T(8,128)S(1)}, u32[]{:S(2)}) %copy-start) | copy-done | bytes 29360152
  775.9 4.4 multiply_reduce_fusion.2
  780.3 0.0 copy-done.2
  780.3 0.3 multiply_add_fusion.1
  780.6 10.4 %sub.38 = f32[16,224,2048]{2,1,0:T(8,128)} broadcast(f32[224,2048]{1,0:T(8,128)S(1)} %multiply_add_fusion.1), dimensions={1,2} | broadcast | bytes 31195136 | tf_op jit(solution)/shard_map/sub | solution.py:23
  791.0 42.5 %sub.39 = f32[1,3584,2048]{2,0,1:T(1,128)} reshape(f32[16,224,2048]{2,1,0:T(8,128)} %sub.38) | data formatting | bytes 58720256 | tf_op jit(solution)/shard_map/sub | solution.py:23
  833.6 45.4 %multiply_reduce_fusion.1 = f32[3584]{0:T(1024)S(1)} fusion(f32[1,3584,2048]{2,0,1:T(1,128)} %all-to-all-done, f32[1,3584,2048]{2,0,1:T(1,128)} %sub.39), kind=kLoop, calls=%fused_computation.1 | loop fusion | flops 22016512 | bytes 58734592 | tf_op jit(solution)/shard_map/reduce_sum | solution.py:24
  879.0 0.1 reduce_sum.55
  879.0 0.1 reduce_sum.56
  879.2 41.8 %psum.15 = f32[16]{0:T(128)S(1)} all-reduce(f32[16]{0:T(128)S(1)} %reduce_sum.56), channel_id=1, replica_groups=mesh['worker'=4,'outer'=4,'mp'=2] {'worker','outer','mp'}, use_global_device_ids=true, to_apply=%region_6.7 | all-reduce | flops 16 | bytes 128 | tf_op jit(solution)/shard_map/psum | solution.py:25
  920.9 11.9 %multiply_reduce_fusion = f32[224,2048]{1,0:T(8,128)S(1)} fusion(f32[16,224,2048]{2,1,0:T(8,128)} %bitcast.5, f32[16]{0:T(128)S(1)} %multiply_minimum_fusion, f32[224,2048]{1,0:T(8,128)S(1)} %multiply_add_fusion.1), kind=kLoop, calls=%fused_computation | loop fusion | flops 21561344 | bytes 33030208 | tf_op jit(solution)/shard_map/reduce_sum | solution.py:27
  932.8 1.5 multiply_add_fusion
  (2 shorter events, 0.0 us)
Async XLA Ops:
  23.7 8.2 copy-start.1
  23.7 641.2 %all-to-all-start = ((f32[1,3584,2048]{2,0,1:T(1,128)}), f32[1,3584,2048]{2,0,1:T(1,128)}, u32[]{:S(2)}, u32[]{:S(2)}) async-start(f32[1,3584,2048]{2,0,1:T(1,128)} %reshape.36), calls=%async_computation | async-start | bytes 58720256 | tf_op jit(solution)/shard_map/all_to_all | solution.py:21
  765.6 10.3 %copy-start = (f32[1,3584,2048]{2,1,0:T(8,128)}, f32[1,3584,2048]{2,1,0:T(8,128)S(1)}, u32[]{:S(2)}) copy-start(f32[1,3584,2048]{2,1,0:T(8,128)S(1)} %copy.4) | copy-start | bytes 88080384
  765.6 14.7 %copy-start.2 = (f32[224,2048]{1,0:T(8,128)S(1)}, f32[224,2048]{1,0:T(8,128)}, u32[]{:S(2)}) copy-start(f32[224,2048]{1,0:T(8,128)} %param.4) | copy-start | bytes 5505028
where the time goes:
time: 937 us; the launch traced here: 934 us
  waiting for transfers between devices  580 us (62%)
  local copies, waits for them, and re-layouts  158 us (17%)
  other arithmetic  109 us (12%)
  blocking collectives  79.2 us (8%)
    all_to_all x1, waiting for transfers between devices, on_device(): lax.all_to_all(mine, ('worker', 'outer'), split_axis=1, concat_axis=0, ti...  580 us
    sub x4, local copies, waits for them, and re-layouts, on_device(): difference = gathered - own_rows[None]  106 us
    reduce_sum x4, other arithmetic, on_device(): partial_value = jnp.sum(difference * difference, axis=(1, 2))  91.1 us
    psum x2, blocking collectives, on_device(): norm_sq = lax.psum(partial_value, ('worker', 'outer', 'mp'))  79.2 us
    unnamed x7, local copies, waits for them, and re-layouts  28 us
    reshape x1, local copies, waits for them, and re-layouts, on_device(): mine = grads.reshape(1, grads.shape[2], grads.shape[3])  23.7 us
  transfers between devices with their start and end apart: 1, of which 1 were waited for; matrix products, arithmetic and copies ran while one was open for 6% of the time, Pallas kernels for 0%

commit v1 on v0

--- a/solution.py
+++ b/solution.py
@@ -8,21 +8,31 @@
 D = 3584
 ITERS = 2
 KVW = 4096
+AXES = ("worker", "outer", "mp")
+
+epsilon = 1e-06
 
 
-epsilon = 1e-06
+def sum_over_devices(value):
+    for axis in AXES:
+        size = lax.axis_size(axis)
+        step = 1
+        while step < size:
+            value = value + lax.ppermute(value, axis, [(i, i ^ step) for i in range(size)])
+            step *= 2
+    return value
 
 
 def on_device(grads, center, radius):
     worker_count = lax.axis_size("worker") * lax.axis_size("outer")
     radius_total = radius[0] * math.sqrt(D * KVW)
     own_rows = center
-    mine = grads.reshape(1, grads.shape[2], grads.shape[3])
-    gathered = lax.all_to_all(mine, ("worker", "outer"), split_axis=1, concat_axis=0, tiled=True)
+    mine = grads.reshape(worker_count, grads.shape[2] // worker_count, grads.shape[3])
+    gathered = lax.all_to_all(mine, ("worker", "outer"), split_axis=0, concat_axis=0, tiled=True)
     for iteration in range(ITERS):
         difference = gathered - own_rows[None]
         partial_value = jnp.sum(difference * difference, axis=(1, 2))
-        norm_sq = lax.psum(partial_value, ("worker", "outer", "mp"))
+        norm_sq = sum_over_devices(partial_value)
         factor = jnp.minimum(1.0, radius_total * lax.rsqrt(norm_sq + epsilon))
         summed = jnp.sum(factor[:, None, None] * difference, axis=0)
         own_rows = own_rows + summed / worker_count

time: 937 us -> 694 us (0.74)
  blocking collectives: 79.2 us -> 642 us
  waiting for transfers between devices: 580 us -> 27.7 us
  local copies, waits for them, and re-layouts: 158 us -> 0.01 us
  other arithmetic: 109 us -> 19.6 us
    all_to_all x0 -> x1, blocking collectives: none -> 642 us  [on_device(): lax.all_to_all(mine, ('worker', 'outer'), split_axis=0, concat_axis=0, ti...]
    all_to_all x1 -> x0, waiting for transfers between devices: 580 us -> none  [on_device(): lax.all_to_all(mine, ('worker', 'outer'), split_axis=1, concat_axis=0, ti...]
    sub x4 -> x0, local copies, waits for them, and re-layouts: 106 us -> none  [on_device(): difference = gathered - own_rows[None]]
    reduce_sum x4 -> x2, other arithmetic: 91.1 us -> 8.95 us  [on_device(): partial_value = jnp.sum(difference * difference, axis=(1, 2))]
    psum x2 -> x0, blocking collectives: 79.2 us -> none  [on_device(): norm_sq = lax.psum(partial_value, ('worker', 'outer', 'mp'))]
    unnamed x7 -> x2, local copies, waits for them, and re-layouts: 28 us -> 0.01 us
    ppermute x0 -> x10, waiting for transfers between devices: none -> 27.7 us  [sum_over_devices(): lax.ppermute(value, axis, [(i, i ^ step) for i in range(size)])]
    reshape x1 -> x0, local copies, waits for them, and re-layouts: 23.7 us -> none  [on_device(): mine = grads.reshape(1, grads.shape[2], grads.shape[3])]
  transfers between devices with their start and end apart: 1 -> 10, of which waited for: 1 -> 10; matrix products, arithmetic and copies ran while one was open for 6% -> 0% of each run, Pallas kernels for 0% -> 0%
where the time goes in v1:
time: 694 us
  blocking collectives  642 us (93%)
  waiting for transfers between devices  27.7 us (4%)
  other arithmetic  19.6 us (3%)
    all_to_all x1, blocking collectives, on_device(): lax.all_to_all(mine, ('worker', 'outer'), split_axis=0, concat_axis=0, ti...  642 us
    ppermute x10, waiting for transfers between devices, sum_over_devices(): lax.ppermute(value, axis, [(i, i ^ step) for i in range(size)])  27.7 us
  transfers between devices with their start and end apart: 10, of which 10 were waited for; matrix products, arithmetic and copies ran while one was open for 0% of the time, Pallas kernels for 0%

profile of v1, /device:TPU:0, one launch (start us, length us, event | category | flops | bytes accessed | tf_op | source)
XLA Modules:
  0.0 694.2 jit_solution(6370008539968846351)
XLA Ops:
  0.0 0.0 copy-start
  0.0 641.9 %all_to_all.5 = f32[16,224,2048]{2,1,0:T(8,128)S(1)} all-to-all(f32[16,224,2048]{2,1,0:T(8,128)} %bitcast.2), channel_id=1, replica_groups=mesh['worker'=4,'outer'=4,'mp'=2] {'worker','outer'}, dimensions={0} | all-to-all | bytes 58720256 | tf_op jit(solution)/shard_map/all_to_all | solution.py:31
  641.9 0.0 copy-done
  641.9 4.5 multiply_reduce_fusion.3
  646.3 0.0 collective-permute-start
  646.4 1.1 collective-permute-done
  647.5 0.6 collective-permute-start.1
  648.1 3.0 collective-permute-done.1
  651.1 0.0 collective-permute-start.2
  651.1 3.6 collective-permute-done.2
  654.7 0.0 collective-permute-start.3
  655.3 3.8 collective-permute-done.3
  659.1 1.5 collective-permute-start.4
  660.7 2.0 collective-permute-done.4
  662.7 4.4 multiply_reduce_fusion.2
  667.1 0.3 multiply_add_fusion.1
  667.5 4.5 multiply_reduce_fusion.1
  671.9 0.0 collective-permute-start.5
  672.0 1.1 collective-permute-done.5
  673.1 0.6 collective-permute-start.6
  673.7 3.0 collective-permute-done.6
  676.7 0.0 collective-permute-start.7
  676.7 3.6 collective-permute-done.7
  680.3 0.0 collective-permute-start.8
  680.3 4.5 collective-permute-done.8
  684.7 1.5 collective-permute-start.9
  686.3 2.0 collective-permute-done.9
  688.3 4.4 multiply_reduce_fusion
  692.7 1.5 multiply_add_fusion
  (10 shorter events, 0.0 us)
Async XLA Ops:
  0.0 641.9 %copy-start = (f32[224,2048]{1,0:T(8,128)S(1)}, f32[224,2048]{1,0:T(8,128)}, u32[]{:S(2)}) copy-start(f32[224,2048]{1,0:T(8,128)} %param.4) | copy-start | bytes 5505028
  646.3 1.2 collective-permute-start
  647.5 3.6 collective-permute-start.1
  651.1 3.6 collective-permute-start.2
  654.7 4.5 collective-permute-start.3
  659.1 3.6 collective-permute-start.4
  671.9 1.2 collective-permute-start.5
  673.1 3.6 collective-permute-start.6
  676.7 3.6 collective-permute-start.7
  680.3 4.5 collective-permute-start.8
  684.7 3.6 collective-permute-start.9
